TPU v7x, 32 devices: a whole 2x2x4 slice. The times are simulated.
32 devices in a mesh: atom: 16 (over z, x, core), chan: 2 (over y).
Axes of the slice: x: 2, y: 2, z: 4, core: 2. Of those that a mesh axis runs over, the one named last changes fastest.
Arguments:
- positions: float32 [3, 2048], P(None, 'atom'), may hold values from -9 to 9
- features: bfloat16 [512, 2048], P('chan', 'atom'), may hold values from -6 to 6
- struct_ids: int32 [2048], P('atom'), may hold values from 0 to 15, as said below
- slots: int32 [64, 2048], P(None, 'atom'), may hold values from 0 to 96, as said below
- validity: int32 [64, 2048], P(None, 'atom'), may hold values from 0 to 1, as said below
- radial_in: bfloat16 [512, 128], replicated, may hold values from -72 to 72
- radial_out: bfloat16 [512, 512], P('chan'), may hold values from -0.0234375 to 0.0234375
- mixing: bfloat16 [512, 512], P(None, 'chan'), may hold values from -0.5 to 0.5
- readout: float32 [512], replicated, may hold values from -0.0078125 to 0.0078125
Outputs:
- forces: float32 [3, 2048], P(None, 'atom')
- stress: float32 [9, 16], replicated
Inputs may be any that keep to these rules, and one draw needn't show every extreme that they name: `struct_ids`: structure numbers never fall along the atoms and every structure has at least one atom. `slots`: the 64 slot values of one atom are distinct and never equal 48. `validity`: an edge is valid only where its neighbour atom exists and belongs to the same structure.
All inputs are finite; a program needn't handle non-finite values.
Results may differ from a plain program's by a relative error of at most 0.0099.
Values may be sent and summed in bfloat16 or wider, within the bound.
A program may use at most 64 MiB of HBM per device.

v0:
```python
import jax
import jax.numpy as jnp
from jax import lax
from jax.sharding import PartitionSpec as P

RIM = 48


sharpness = 40.0
reach = 10.0


def with_halo(value, sides, width):
    for axis, dim in sides:
        size, length = (lax.axis_size(axis), value.shape[dim])
        up = [(i, (i + 1) % size) for i in range(size - 1)]
        down = [(j, i) for i, j in up]
        last = lax.slice_in_dim(value, length - width, length, axis=dim)
        first = lax.slice_in_dim(value, 0, width, axis=dim)
        before = lax.ppermute(last, axis, up)
        after = lax.ppermute(first, axis, down)
        value = jnp.concatenate([before, value, after], axis=dim)
    return value


def from_behind(value, axis, by):
    size = lax.axis_size(axis)
    pairs = [(i, i + by) for i in range(size) if 0 <= i + by < size]
    return lax.ppermute(value, axis, pairs)


def dsilu(value):
    sigma = jax.nn.sigmoid(value)
    return sigma * (1.0 + value * (1.0 - sigma))


def radial_terms(vector, radial_in, radial_out):
    dist = jnp.sqrt(1.0 + jnp.sum(vector * vector, axis=0))
    count = radial_in.shape[1]
    centers = jnp.arange(count).astype(jnp.float32) * (reach / count)
    offset = dist[None, :] - centers[:, None]
    bump = jnp.exp(-sharpness * offset * offset)
    basis = bump.astype(jnp.bfloat16)
    slope = (-2.0 * sharpness * offset * bump).astype(jnp.bfloat16)
    pre = jnp.dot(radial_in, basis, preferred_element_type=jnp.float32)
    dpre = jnp.dot(radial_in, slope, preferred_element_type=jnp.float32)
    hidden = jax.nn.silu(pre).astype(jnp.bfloat16)
    dhidden = (dsilu(pre) * dpre).astype(jnp.bfloat16)
    radial = jnp.dot(radial_out, hidden, preferred_element_type=jnp.float32)
    dradial = jnp.dot(radial_out, dhidden, preferred_element_type=jnp.float32)
    return (dist, radial, dradial)


def local(positions, features, struct_ids, slots, validity, radial_in, radial_out, mixing, readout):
    slot_count, atom_count = slots.shape
    padded_feat, padded_pos = (
        with_halo(features.astype(jnp.float32), (("atom", 1),), RIM).astype(features.dtype),
        with_halo(positions, (("atom", 1),), RIM),
    )
    atom_index = jnp.arange(atom_count, dtype=jnp.int32)
    whole_feat, whole_radial, whole_mix = (
        lax.all_gather(padded_feat, "chan", axis=0, tiled=True),
        lax.all_gather(radial_out, "chan", axis=0, tiled=True),
        lax.all_gather(mixing, "chan", axis=1, tiled=True),
    )
    used = slot_count // lax.axis_size("chan")
    first = lax.axis_index("chan") * used
    slot_rows = lax.dynamic_slice_in_dim(slots, first, used, 0)
    valid_rows = lax.dynamic_slice_in_dim(validity, first, used, 0)
    flat_index = (atom_index[None, :] + slot_rows).reshape(-1)
    far_feat = whole_feat[:, flat_index]
    vector = padded_pos[:, flat_index] - jnp.tile(positions, (1, used))
    weight = valid_rows.reshape(-1).astype(jnp.float32)
    dist, radial, dradial = radial_terms(vector, radial_in, whole_radial)
    message = (far_feat * radial).astype(jnp.bfloat16)
    mixed = jnp.dot(whole_mix, message, preferred_element_type=jnp.float32)
    gmix = (weight[None, :] * readout[:, None] * dsilu(mixed)).astype(jnp.bfloat16)
    gmsg = lax.dot_general(
        whole_mix, gmix, (((0,), (0,)), ((), ())), preferred_element_type=jnp.float32
    )
    gdist = jnp.sum(gmsg * far_feat.astype(jnp.float32) * dradial, axis=0)
    gvec = gdist * vector / dist
    outgoing = gvec.reshape(3, used, atom_count).sum(axis=1)
    table = jnp.zeros((3, atom_count + 2 * RIM), jnp.float32).at[:, flat_index].add(-gvec)
    table = table.at[:, RIM : RIM + atom_count].add(outgoing)
    atomvir = (vector[:, None, :] * gvec[None, :, :]).reshape(9, used, atom_count).sum(axis=1)
    table, atomvir = lax.psum((table, atomvir), "chan")
    from_next = from_behind(table[:, :RIM], "atom", -1)
    from_prior = from_behind(table[:, RIM + atom_count :], "atom", 1)
    forces = table[:, RIM : RIM + atom_count]
    forces = forces + jnp.pad(from_prior, ((0, 0), (0, atom_count - RIM)))
    forces = forces + jnp.pad(from_next, ((0, 0), (atom_count - RIM, 0)))
    struct_total = atom_count * lax.axis_size("atom") // 128
    onehot = (struct_ids[None, :] == jnp.arange(struct_total, dtype=jnp.int32)[:, None]).astype(
        jnp.float32
    )
    virial = jnp.dot(atomvir, onehot.T, precision=lax.Precision.HIGHEST)
    counts = jnp.sum(onehot, axis=1)
    virial, counts = lax.psum((virial, counts), "atom")
    stress = -virial / counts[None, :]
    return (forces, stress)


def solution(mesh):
    placed = (
        P(None, "atom"),
        P("chan", "atom"),
        P("atom"),
        P(None, "atom"),
        P(None, "atom"),
        P(),
        P("chan", None),
        P(None, "chan"),
        P(),
    )
    return jax.shard_map(
        local, mesh=mesh, in_specs=placed, out_specs=(P(None, "atom"), P()), check_vma=False
    )
```

profile of v0, /device:TPU:0, one launch (start us, length us, event | category | flops | bytes accessed | tf_op | source)
XLA Modules:
  0.0 178.9 jit_solution(14820634431349806464)
XLA Ops:
  0.6 0.8 fusion.61
  1.5 1.3 collective-permute-start.3
  2.8 3.0 %collective-permute-start.2 = (f32[3,48]{1,0:T(4,128)S(1)}, f32[3,48]{1,0:T(4,128)S(1)}, u32[]{:S(2)}, u32[]{:S(2)}) collective-permute-start(f32[3,48]{1,0:T(4,128)S(1)} %get-tuple-element.38), channel_id=1, source_target_pairs={{0,2},{2,4},{4,6},{6,8},{8,10},{10,12},{12,14},{14,16},{16,18},{18... | collective-permute-start | bytes 1736 | tf_op jit(solution)/shard_map/ppermute | solution.py:20
  5.8 0.9 copy.46
  6.8 0.7 fusion.60
  7.4 1.3 collective-permute-start.1
  8.7 5.7 %collective-permute-start = (bf16[256,48]{0,1:T(8,128)(2,1)}, bf16[256,48]{0,1:T(8,128)(2,1)}, u32[]{:S(2)}, u32[]{:S(2)}) collective-permute-start(bf16[256,48]{0,1:T(8,128)(2,1)} %get-tuple-element.34), channel_id=1, source_target_pairs={{0,2},{2,4},{4,6},{6,8},{8,10},{10,12},{12,14},{14,16},{16,18},{18... | collective-permute-start | bytes 73736 | tf_op jit(solution)/shard_map/ppermute | solution.py:20
  14.4 0.7 broadcast_bitcast_fusion
  15.1 0.7 dynamic-slice_add_fusion
  16.5 9.9 %all_gather.11 = bf16[512,512]{1,0:T(8,128)(2,1)S(1)} all-gather(bf16[512,256]{1,0:T(8,128)(2,1)} %param.18), channel_id=1, replica_groups=mesh['atom'=16,'chan'=2] {'chan'}, dimensions={1}, use_global_device_ids=true | all-gather | bytes 786432 | tf_op jit(solution)/shard_map/all_gather | solution.py:64
  26.3 1.3 convert_bitcast_fusion
  27.6 9.2 %all_gather.10 = bf16[512,512]{1,0:T(8,128)(2,1)S(1)} all-gather(bf16[256,512]{1,0:T(8,128)(2,1)} %param.17), channel_id=1, replica_groups=mesh['atom'=16,'chan'=2] {'chan'}, dimensions={0}, use_global_device_ids=true | all-gather | bytes 786432 | tf_op jit(solution)/shard_map/all_gather | solution.py:63
  36.8 0.8 convert_reduce_fusion
  37.6 0.6 compare_reduce_fusion
  38.3 0.8 pad_maximum_fusion.1
  39.2 10.8 %gather_fusion.1 = f32[4096,3]{1,0:T(8,128)S(1)} fusion(f32[3,224]{0,1:T(8,128)S(1)} %copy.48, s32[4096]{0:T(1024)S(1)} %broadcast_clamp_fusion), kind=kCustom, calls=%fused_computation.1 | custom fusion | bytes 114688 | tf_op jit(solution)/shard_map/gather | solution.py:72
  50.0 0.6 copy.49
  50.7 4.6 %fusion.28 = f32[4096,512]{1,0:T(8,128)} fusion(bf16[512,128]{1,0:T(8,128)(2,1)S(1)} %copy-done, f32[128]{0:T(128)S(1)} %convert_multiply_fusion.2, f32[4096]{0:T(1024)S(1)} %get-tuple-element.37), kind=kOutput, calls=%fused_computation.37 | convolution fusion | flops 538968064 | bytes 8536576 | tf_op jit(solution)/shard_map/dot_general | solution.py:45
  55.3 0.8 pad_maximum_fusion
  56.1 5.6 %all_gather.9 = bf16[512,224]{0,1:T(8,128)(2,1)S(1)} all-gather(bf16[256,224]{0,1:T(8,128)(2,1)S(1)} %pad_maximum_fusion), channel_id=1, replica_groups=mesh['atom'=16,'chan'=2] {'chan'}, dimensions={0}, use_global_device_ids=true | all-gather | bytes 344064 | tf_op jit(solution)/shard_map/all_gather | solution.py:62
  61.7 17.3 %gather_fusion = bf16[4096,512]{1,0:T(8,128)(2,1)} fusion(bf16[512,224]{0,1:T(8,128)(2,1)S(1)} %all_gather.9, s32[4096]{0:T(1024)S(1)} %broadcast_clamp_fusion), kind=kCustom, calls=%fused_computation | custom fusion | bytes 8404992 | tf_op jit(solution)/shard_map/gather | solution.py:71
  79.0 9.5 %fusion.2 = bf16[4096,512]{1,0:T(8,128)(2,1)} fusion(bf16[4096,512]{1,0:T(8,128)(2,1)} %gather_fusion, bf16[512,512]{1,0:T(8,128)(2,1)S(1)} %all_gather.10, f32[4096,512]{1,0:T(8,128)} %fusion.28), kind=kOutput, calls=%fused_computation.7 | convolution fusion | flops 2164260864 | bytes 17301504 | tf_op jit(solution)/shard_map/dot_general | solution.py:49
  88.4 9.6 %fusion.18 = f32[4096,512]{1,0:T(8,128)} fusion(bf16[512,512]{1,0:T(8,128)(2,1)S(1)} %all_gather.11, f32[512]{0:T(512)S(1)} %copy-done.7, f32[4096]{0:T(1024)S(1)} %copy-done.5, bf16[4096,512]{1,0:T(8,128)(2,1)} %fusion.2), kind=kOutput, calls=%fused_computation.28 | convolution fusion | flops 4315938816 | bytes 13125632 | tf_op jit(solution)/shard_map/dot_general | solution.py:78
  98.0 9.7 %fusion.1 = f32[4096]{0:T(1024)S(1)} fusion(f32[4096,512]{1,0:T(8,128)} %fusion.18, bf16[4096,512]{1,0:T(8,128)(2,1)} %gather_fusion, bf16[512,512]{1,0:T(8,128)(2,1)S(1)} %all_gather.10, f32[4096,512]{1,0:T(8,128)} %fusion.28, bf16[512,128]{1,0:T(8,128)(2,1)S(1)} %copy-done, f32[128]{0:T(128)S(1)} %convert_multiply_fusion.2, f32[4096]{0:T(1024)S(1)} %get-tuple-element.37), kind=kOutput, calls=%fused_computation.6 | convolution fusion | flops 2714759168 | bytes 21660160 | tf_op jit(solution)/shard_map/dot_general | solution.py:50
  107.8 0.6 copy.52
  108.8 22.5 %scatter_custom_fusion = f32[3,224]{0,1:T(8,128)S(1)} fusion(s32[4096]{0:T(1024)} %bitcast.88, f32[4096,3]{1,0:T(8,128)S(1)} %copy.52, f32[]{:T(128)} %constant.45.clone.1), kind=kCustom, calls=%fused_computation.56 | custom fusion | flops 12288 | bytes 3200 | tf_op jit(solution)/shard_map/scatter-add | solution.py:84
  131.3 0.7 fusion.41
  132.0 9.6 %all-reduce.3 = (f32[3,224]{0,1:T(8,128)S(1)}, f32[9,128]{1,0:T(8,128)S(1)}) all-reduce(f32[3,224]{0,1:T(8,128)S(1)} %fusion.41, f32[9,128]{1,0:T(8,128)S(1)} %reduce_sum.48), channel_id=1, replica_groups=mesh['atom'=16,'chan'=2] {'chan'}, use_global_device_ids=true, to_apply=%region_5.6 | all-reduce | flops 1824 | bytes 14592 | tf_op jit(solution)/shard_map/psum | solution.py:87
  141.6 1.3 collective-permute-start.5
  142.9 3.0 %collective-permute-start.4 = (f32[3,48]{0,1:T(8,128)S(1)}, f32[3,48]{0,1:T(8,128)S(1)}, u32[]{:S(2)}, u32[]{:S(2)}) collective-permute-start(f32[3,48]{0,1:T(8,128)S(1)} %get-tuple-element.32), channel_id=1, source_target_pairs={{0,2},{2,4},{4,6},{6,8},{8,10},{10,12},{12,14},{14,16},{16,18},{18... | collective-permute-start | bytes 1736 | tf_op jit(solution)/shard_map/ppermute | solution.py:29
  146.0 31.6 %all-reduce.2 = (f32[9,16]{1,0:T(8,128)S(1)}, f32[16]{0:T(128)S(1)}) all-reduce(f32[9,16]{1,0:T(8,128)S(1)} %fusion.48, f32[16]{0:T(128)S(1)} %convert_reduce_fusion), channel_id=1, replica_groups=mesh['atom'=16,'chan'=2] {'atom'}, use_global_device_ids=true, to_apply=%region_8.9 | all-reduce | flops 160 | bytes 1280 | tf_op jit(solution)/shard_map/psum | solution.py:99
  178.3 0.7 copy.54
  (38 shorter events, 2.0 us)
Async XLA Ops:
  0.6 50.1 %copy-start = (bf16[512,128]{1,0:T(8,128)(2,1)S(1)}, bf16[512,128]{1,0:T(8,128)(2,1)}, u32[]{:S(2)}) copy-start(bf16[512,128]{1,0:T(8,128)(2,1)} %param.16) | copy-start | bytes 393220
  1.5 36.8 %collective-permute-start.3 = (f32[3,48]{1,0:T(4,128)S(1)}, f32[3,48]{1,0:T(4,128)S(1)}, u32[]{:S(2)}, u32[]{:S(2)}) collective-permute-start(f32[3,48]{1,0:T(4,128)S(1)} %get-tuple-element.39), channel_id=1, source_target_pairs={{2,0},{4,2},{6,4},{8,6},{10,8},{12,10},{14,12},{16,14},{18,16},{20... | collective-permute-start | bytes 1736 | tf_op jit(solution)/shard_map/ppermute | solution.py:21
  2.8 35.5 %collective-permute-start.2 = (f32[3,48]{1,0:T(4,128)S(1)}, f32[3,48]{1,0:T(4,128)S(1)}, u32[]{:S(2)}, u32[]{:S(2)}) collective-permute-start(f32[3,48]{1,0:T(4,128)S(1)} %get-tuple-element.38), channel_id=1, source_target_pairs={{0,2},{2,4},{4,6},{6,8},{8,10},{10,12},{12,14},{14,16},{16,18},{18... | collective-permute-start | bytes 1736 | tf_op jit(solution)/shard_map/ppermute | solution.py:20
  6.7 31.5 %copy-start.1 = (bf16[256,128]{0,1:T(8,128)(2,1)}, bf16[256,128]{0,1:T(8,128)(2,1)S(1)}, u32[]{:S(2)}) copy-start(bf16[256,128]{0,1:T(8,128)(2,1)S(1)} %copy.46) | copy-start | bytes 196612
  7.4 47.9 %collective-permute-start.1 = (bf16[256,48]{0,1:T(8,128)(2,1)}, bf16[256,48]{0,1:T(8,128)(2,1)}, u32[]{:S(2)}, u32[]{:S(2)}) collective-permute-start(bf16[256,48]{0,1:T(8,128)(2,1)} %get-tuple-element.35), channel_id=1, source_target_pairs={{2,0},{4,2},{6,4},{8,6},{10,8},{12,10},{14,12},{16,14},{18,16},{20... | collective-permute-start | bytes 73736 | tf_op jit(solution)/shard_map/ppermute | solution.py:21
  8.7 46.6 %collective-permute-start = (bf16[256,48]{0,1:T(8,128)(2,1)}, bf16[256,48]{0,1:T(8,128)(2,1)}, u32[]{:S(2)}, u32[]{:S(2)}) collective-permute-start(bf16[256,48]{0,1:T(8,128)(2,1)} %get-tuple-element.34), channel_id=1, source_target_pairs={{0,2},{2,4},{4,6},{6,8},{8,10},{10,12},{12,14},{14,16},{16,18},{18... | collective-permute-start | bytes 73736 | tf_op jit(solution)/shard_map/ppermute | solution.py:20
  15.9 0.6 copy-start.3
  49.9 5.3 %copy-start.2 = (bf16[256,128]{0,1:T(8,128)(2,1)S(1)}, bf16[256,128]{0,1:T(8,128)(2,1)}, u32[]{:S(2)}) copy-start(bf16[256,128]{0,1:T(8,128)(2,1)} %copy-done.1) | copy-start | bytes 196612
  79.0 9.5 %copy-start.5 = (f32[4096]{0:T(1024)S(1)}, f32[4096]{0:T(1024)}, u32[]{:S(2)}) copy-start(f32[4096]{0:T(1024)} %convert_bitcast_fusion) | copy-start | bytes 49156
  79.0 9.5 %copy-start.7 = (f32[512]{0:T(512)S(1)}, f32[512]{0:T(512)}, u32[]{:S(2)}) copy-start(f32[512]{0:T(512)} %param.19) | copy-start | bytes 6148
  98.0 10.4 %copy-start.4 = (f32[3,128]{1,0:T(4,128)S(1)}, f32[3,128]{1,0:T(4,128)}, u32[]{:S(2)}) copy-start(f32[3,128]{1,0:T(4,128)} %param.11) | copy-start | bytes 4612
  98.0 47.8 %copy-start.6 = (s32[128]{0:T(128)S(1)}, s32[128]{0:T(128)}, u32[]{:S(2)}) copy-start(s32[128]{0:T(128)} %param.13) | copy-start | bytes 1540
  141.6 36.7 %collective-permute-start.5 = (f32[3,48]{0,1:T(8,128)S(1)}, f32[3,48]{0,1:T(8,128)S(1)}, u32[]{:S(2)}, u32[]{:S(2)}) collective-permute-start(f32[3,48]{0,1:T(8,128)S(1)} %get-tuple-element.33), channel_id=1, source_target_pairs={{2,0},{4,2},{6,4},{8,6},{10,8},{12,10},{14,12},{16,14},{18,16},{20... | collective-permute-start | bytes 1736 | tf_op jit(solution)/shard_map/ppermute | solution.py:29
  142.9 35.4 %collective-permute-start.4 = (f32[3,48]{0,1:T(8,128)S(1)}, f32[3,48]{0,1:T(8,128)S(1)}, u32[]{:S(2)}, u32[]{:S(2)}) collective-permute-start(f32[3,48]{0,1:T(8,128)S(1)} %get-tuple-element.32), channel_id=1, source_target_pairs={{0,2},{2,4},{4,6},{6,8},{8,10},{10,12},{12,14},{14,16},{16,18},{18... | collective-permute-start | bytes 1736 | tf_op jit(solution)/shard_map/ppermute | solution.py:29
where the time goes:
time: 180 us; the launch traced here: 179 us
  blocking collectives  65.9 us (37%)
  local copies, waits for them, and re-layouts  34 us (19%)
  matrix products  33.5 us (19%)
  other arithmetic  29 us (16%)
  starting transfers between devices  15.6 us (9%)
    psum x1, blocking collectives, local(): virial, counts = lax.psum((virial, counts), 'atom')  31.6 us
    scatter-add x1, other arithmetic, local(): jnp.zeros((3, atom_count + 2 * RIM), jnp.float32).at[:, flat_index]  22.5 us
    gather x1, local copies, waits for them, and re-layouts, local(): far_feat = whole_feat[:, flat_index]  17.3 us
    gather x2, local copies, waits for them, and re-layouts, local(): vector = padded_pos[:, flat_index] - jnp.tile(positions, (1, used))  11.4 us
    all_gather x1, blocking collectives, local(): lax.all_gather(mixing, 'chan', axis=1, tiled=True)  9.87 us
    dot_general x1, matrix products, radial_terms(): dradial = jnp.dot(radial_out, dhidden, preferred_element_type=jnp.float32)  9.7 us
    dot_general x1, matrix products, local(): lax.dot_general(whole_mix, gmix, (((0,), (0,)), ((), ())), preferred_elem...  9.6 us
    psum x1, blocking collectives, local(): table, atomvir = lax.psum((table, atomvir), 'chan')  9.57 us
  transfers between devices with their start and end apart: 6, of which 0 were waited for; matrix products, arithmetic and copies ran while one was open for 13% of the time, Pallas kernels for 0%

commit v1 on v0

v1 whole, which is shorter than its diff:
```python
import functools

import jax
import jax.numpy as jnp
from jax import lax
from jax.experimental import pallas as pl
from jax.experimental.pallas import tpu as pltpu
from jax.sharding import PartitionSpec as P

RIM = 48
sharpness = 40.0
reach = 10.0
F32 = jnp.float32
BF16 = jnp.bfloat16
TILE = 256
MESH = pl.DeviceIdType.MESH


def dot(a, b):
    return jnp.dot(a, b, preferred_element_type=F32)


def sigmoid(value):
    return 0.5 * jnp.tanh(0.5 * value) + 0.5


def kernel(
    size,
    structs,
    pos,
    feat,
    sid,
    slots,
    valid,
    r_in,
    r_out,
    mix,
    readout,
    forces,
    stress,
    fwin,
    pnbr,
    ro_r,
    mix_r,
    mix_t,
    pwin,
    own_pos,
    idx_s,
    w_s,
    hot_s,
    vec_s,
    dist_s,
    hid_s,
    dhid_s,
    mixp_s,
    fd_s,
    acc,
    gsum,
    avir,
    tab_own,
    tab_nbr,
    tabs,
    part,
    parts,
    total,
    totals,
    pos_sems,
    nbr_sems,
    own_sems,
    ro_sems,
    mix_sems,
    psems,
    tsems,
):
    a, c = lax.axis_index("atom"), lax.axis_index("chan")
    channels, atoms = feat.shape
    n = readout.shape[1] // channels
    half = atoms // n
    rows = slots.shape[0] // n
    group = 4 if size % 4 == 0 else 1
    deep = size // group
    place, z = lax.rem(a, group), lax.div(a, group)
    before, after = lax.rem(a + size - 1, size), lax.rem(a + 1, size)

    def at(atom, chan):
        return {"atom": atom, "chan": chan}

    plane = []
    for step in range(1, n * group):
        spot = lax.rem(place * n + c + step, n * group)
        plane.append((z * group + lax.div(spot, n), lax.rem(spot, n)))
    line = [(lax.rem(z + step, deep) * group + place, c) for step in range(1, deep)]
    ends = [(side, chan) for side in (before, after) for chan in range(n)]
    others = [(k, lax.rem(c + k, n)) for k in range(1, n)]
    early = c < n // 2

    barrier = pltpu.get_barrier_semaphore()
    for atom, chan in plane + line + ends:
        pl.semaphore_signal(barrier, inc=1, device_id=at(atom, chan), device_id_type=MESH)
    pl.semaphore_wait(barrier, len(plane) + len(line) + len(ends))

    def send(src, dst, sem, sem_recv, atom, chan):
        copy = pltpu.make_async_remote_copy(
            src_ref=src,
            dst_ref=dst,
            send_sem=sem,
            recv_sem=sem_recv,
            device_id=at(atom, chan),
            device_id_type=MESH,
        )
        copy.start()
        return copy

    nbr = pl.ds(atoms, atoms)
    own = pl.ds(0, atoms)
    started = [
        send(pos, pnbr, pos_sems.at[0], pos_sems.at[1], jnp.where(early, after, before), c)
    ]
    for chan in range(n):
        rel = lax.rem(c - chan + n, n)
        side = after if chan < n // 2 else before
        started.append(
            send(feat, fwin.at[rel, :, nbr], nbr_sems.at[0, chan], nbr_sems.at[1, rel], side, chan)
        )
    for k, chan in others:
        started.append(
            send(feat, fwin.at[n - k, :, own], own_sems.at[0, k], own_sems.at[1, n - k], a, chan)
        )
    for k, chan in others:
        started.append(send(r_out, ro_r.at[n - k - 1], ro_sems.at[0, k], ro_sems.at[1, n - k], a, chan))
        started.append(send(mix, mix_r.at[n - k - 1], mix_sems.at[0, k], mix_sems.at[1, n - k], a, chan))

    fwin[0, :, 0:atoms] = feat[...]
    lane = lax.broadcasted_iota(jnp.int32, (rows, atoms), 1)

    def fold(value):
        out = value[0:rows, :]
        for q in range(n):
            moved = pltpu.roll(value[q * rows : (q + 1) * rows, :], lax.rem((q - c + n) * half, atoms), 1)
            out = jnp.where((lane >= q * half) & (lane < (q + 1) * half), moved, out)
        return out

    def whole(value):
        out = value
        for q in range(1, n):
            out = out + pltpu.roll(value, q * half, 1)
        return out

    atom_of = c * half + lax.rem(lane, half)
    idx_s[...] = lax.bitwise_and(fold(slots[...]) + atom_of - RIM, 2 * atoms - 1)
    w_s[...] = fold(valid[...]).astype(F32)
    lane8 = lax.broadcasted_iota(jnp.int32, (8, atoms), 1)
    mine = (lane8 >= c * half) & (lane8 < c * half + half)
    own_pos[...] = jnp.zeros_like(own_pos)
    own_pos[0:3, :] = pos[...]
    spread = own_pos[...]
    pwin[...] = jnp.zeros_like(pwin)

    def split(value, columns):
        one = value.astype(BF16).astype(F32)
        two = (value - one).astype(BF16).astype(F32)
        pwin[0:3, columns] = one
        pwin[8:11, columns] = two
        pwin[16:19, columns] = value - one - two

    split(pos[...], slice(0, atoms))
    own_pos[...] = whole(jnp.where(mine, spread, 0.0))
    scale = readout[...]
    mix_t[0:channels, :] = (mix[...].astype(F32).T * scale).astype(BF16)
    acc[...] = jnp.zeros_like(acc)
    gsum[...] = jnp.zeros_like(gsum)
    avir[...] = jnp.zeros_like(avir)

    def landed(dst, sem):
        pltpu.make_async_copy(dst, dst, sem).wait()

    landed(pnbr, pos_sems.at[1])
    landed(fwin.at[0, :, nbr], nbr_sems.at[1, 0])
    split(pnbr[...], slice(atoms, 2 * atoms))
    count = r_in.shape[1]
    wide = TILE // atoms
    own_tile = jnp.concatenate([own_pos[...]] * wide, axis=1)
    steps = rows // wide

    def row(ref, step):
        return jnp.concatenate(
            [ref[pl.ds(step * wide + k, 1), :] for k in range(wide)], axis=1
        )

    def first(step, carry):
        idx = row(idx_s, step)
        spot = lax.broadcasted_iota(jnp.int32, (2 * atoms, TILE), 0)
        hot = jnp.where(spot == idx, 1.0, 0.0).astype(BF16)
        hot_s[step] = hot
        got = dot(pwin[...].astype(BF16), hot)
        vec = got[0:8] + got[8:16] + got[16:24] - own_tile
        vec_s[step] = vec
        dist = jnp.sqrt(1.0 + jnp.sum(vec * vec, axis=0, keepdims=True))
        dist_s[step] = dist
        centers = lax.broadcasted_iota(jnp.int32, (count, TILE), 0).astype(F32) * (reach / count)
        offset = dist - centers
        bump = jnp.exp(-sharpness * offset * offset)
        basis = bump.astype(BF16)
        slope = (-2.0 * sharpness * offset * bump).astype(BF16)
        pre = dot(r_in[...], basis)
        dpre = dot(r_in[...], slope)
        sigma = sigmoid(pre)
        silu = pre * sigma
        hid = silu.astype(BF16)
        dhid = ((sigma + silu * (1.0 - sigma)) * dpre).astype(BF16)
        hid_s[step] = hid
        dhid_s[step] = dhid
        far = dot(fwin[0], hot)
        message = (far * dot(r_out[...], hid)).astype(BF16)
        fd_s[step] = far * dot(r_out[...], dhid)
        mixp_s[step] = dot(mix[...], message)
        return carry

    lax.fori_loop(0, steps, first, 0)

    for r in range(1, n):
        landed(fwin.at[r, :, nbr], nbr_sems.at[1, r])
        landed(fwin.at[r, :, own], own_sems.at[1, r])
        landed(ro_r.at[r - 1], ro_sems.at[1, r])
        landed(mix_r.at[r - 1], mix_sems.at[1, r])
        mix_t[r * channels : (r + 1) * channels, :] = (
            mix_r[r - 1].astype(F32).T * scale
        ).astype(BF16)
    distant = (n - 1) * channels

    def second(step, carry):
        hot = hot_s[step]
        far = dot(fwin[1:].reshape(distant, 2 * atoms), hot)
        outer = ro_r[...].reshape(distant, ro_r.shape[2])
        message = (far * dot(outer, hid_s[step])).astype(BF16)
        fd = far * dot(outer, dhid_s[step])
        mixed = mixp_s[step]
        for r in range(1, n):
            mixed = mixed + dot(mix_r[r - 1], message[(r - 1) * channels : r * channels])
        sigma = sigmoid(mixed)
        gmix = (sigma + mixed * sigma * (1.0 - sigma)).astype(BF16)
        gmsg = dot(mix_t[...], gmix)
        gdist = jnp.sum(gmsg[0:channels] * fd_s[step], axis=0, keepdims=True) + jnp.sum(
            gmsg[channels:] * fd, axis=0, keepdims=True
        )
        vec = vec_s[step]
        gvec = (row(w_s, step) * gdist / dist_s[step]) * vec
        coarse = gvec.astype(BF16).astype(F32)
        both = jnp.concatenate([coarse, gvec - coarse], axis=0).astype(BF16)
        acc[...] += lax.dot_general(
            both, hot, (((1,), (1,)), ((), ())), preferred_element_type=F32
        )
        sums = gvec[:, 0:atoms]
        for k in range(1, wide):
            sums = sums + gvec[:, k * atoms : (k + 1) * atoms]
        gsum[...] += sums
        for p in range(3):
            term = vec[p : p + 1, :] * gvec
            sums = term[:, 0:atoms]
            for k in range(1, wide):
                sums = sums + term[:, k * atoms : (k + 1) * atoms]
            avir[8 * p : 8 * p + 8, :] += sums
        return carry

    lax.fori_loop(0, steps, second, 0)

    table = acc[0:8, :] + acc[8:16, :]
    tab_own[...] = jnp.where(mine, whole(gsum[...]), 0.0) - table[:, 0:atoms]
    tab_nbr[...] = -table[:, atoms : 2 * atoms]
    side = jnp.where(early, before, after)
    sends = []
    for k, chan in others:
        sends.append(send(tab_own, tabs.at[c], tsems.at[0, k], tsems.at[1, c], a, chan))
    for chan in range(n):
        sends.append(send(tab_nbr, tabs.at[n + c], tsems.at[2, chan], tsems.at[3, c], side, chan))
    tabs[c] = tab_own[...]
    spot = lax.broadcasted_iota(jnp.int32, (atoms, atoms), 0)
    member = jnp.where(spot == sid[...], 1.0, 0.0)
    ones = jnp.where(mine, 1.0, 0.0)
    local = jnp.concatenate([jnp.where(mine, whole(avir[8 * p : 8 * p + 8, :]), 0.0) for p in range(3)] + [ones], axis=0)
    virial = lax.dot_general(
        local, member, (((1,), (1,)), ((), ())), precision=lax.Precision.HIGHEST, preferred_element_type=F32
    )
    part[...] = jnp.zeros_like(part)
    for p in range(4):
        part[3 * p : 3 * p + 3, :] = virial[8 * p : 8 * p + 3, :]
    me = place * n + c
    for k, (atom, chan) in enumerate(plane):
        sends.append(send(part, parts.at[me], psems.at[0, k], psems.at[1, me], atom, chan))
    parts[me] = part[...]
    for k in range(1, n * group):
        spot = lax.rem(me + k, n * group)
        landed(parts.at[spot], psems.at[1, spot])
    summed = parts[0]
    for k in range(1, n * group):
        summed = summed + parts[k]
    total[...] = summed
    for k, (atom, chan) in enumerate(line):
        sends.append(send(total, totals.at[z], psems.at[2, k], psems.at[3, z], atom, chan))
    totals[z] = summed

    for k, chan in others:
        landed(tabs.at[chan], tsems.at[1, chan])
    for chan in range(n):
        landed(tabs.at[n + chan], tsems.at[3, chan])
    force = tabs[0]
    for k in range(1, 2 * n):
        force = force + tabs[k]
    forces[...] = force[0:3, :]

    for k in range(1, deep):
        spot = lax.rem(z + k, deep)
        landed(totals.at[spot], psems.at[3, spot])
    summed = totals[0]
    for k in range(1, deep):
        summed = summed + totals[k]
    out = -summed[0:9, :] / summed[9:10, :]
    stress[...] = out[:, 0:structs]
    for copy in (*started, *sends):
        copy.wait_send()


def local(positions, features, struct_ids, slots, validity, radial_in, radial_out, mixing, readout):
    size = lax.axis_size("atom")
    slot_count, atoms = slots.shape
    structs = atoms * size // 128
    channels, hidden = radial_out.shape
    group = 4 if size % 4 == 0 else 1
    deep = size // group
    n = lax.axis_size("chan")
    steps = slot_count * atoms // n // TILE
    plane = n * group
    vmem = pltpu.VMEM
    dma = pltpu.SemaphoreType.DMA
    return pl.pallas_call(
        functools.partial(kernel, size, structs),
        out_shape=(
            jax.ShapeDtypeStruct((3, atoms), F32),
            jax.ShapeDtypeStruct((9, structs), F32),
        ),
        in_specs=[pl.BlockSpec(memory_space=vmem)] * 9,
        out_specs=(pl.BlockSpec(memory_space=vmem),) * 2,
        scratch_shapes=[
            vmem((n, channels, 2 * atoms), BF16),
            vmem((3, atoms), F32),
            vmem((n - 1, channels, hidden), BF16),
            vmem((n - 1, n * channels, channels), BF16),
            vmem((n * channels, n * channels), BF16),
            vmem((32, 2 * atoms), F32),
            vmem((8, atoms), F32),
            vmem((slot_count // n, atoms), jnp.int32),
            vmem((slot_count // n, atoms), F32),
            vmem((steps, 2 * atoms, TILE), BF16),
            vmem((steps, 8, TILE), F32),
            vmem((steps, 1, TILE), F32),
            vmem((steps, hidden, TILE), BF16),
            vmem((steps, hidden, TILE), BF16),
            vmem((steps, n * channels, TILE), F32),
            vmem((steps, channels, TILE), F32),
            vmem((16, 2 * atoms), F32),
            vmem((8, atoms), F32),
            vmem((24, atoms), F32),
            vmem((8, atoms), F32),
            vmem((8, atoms), F32),
            vmem((2 * n, 8, atoms), F32),
            vmem((16, atoms), F32),
            vmem((plane, 16, atoms), F32),
            vmem((16, atoms), F32),
            vmem((deep, 16, atoms), F32),
            dma((2,)),
            dma((2, n)),
            dma((2, n)),
            dma((2, n)),
            dma((2, n)),
            dma((4, max(plane, deep))),
            dma((4, n)),
        ],
        compiler_params=pltpu.CompilerParams(
            collective_id=0, has_side_effects=True, vmem_limit_bytes=60 * 1024 * 1024
        ),
    )(
        positions,
        features,
        struct_ids.reshape(1, atoms),
        slots,
        validity,
        radial_in,
        radial_out,
        mixing,
        readout.reshape(1, n * channels),
    )


def solution(mesh):
    placed = (
        P(None, "atom"),
        P("chan", "atom"),
        P("atom"),
        P(None, "atom"),
        P(None, "atom"),
        P(),
        P("chan", None),
        P(None, "chan"),
        P(),
    )
    return jax.shard_map(
        local, mesh=mesh, in_specs=placed, out_specs=(P(None, "atom"), P()), check_vma=False
    )
```

time: 180 us -> 54.1 us (0.30)
  blocking collectives: 65.9 us -> 0 us
  Pallas kernels: 0 us -> 50.7 us
  matrix products: 33.5 us -> 0 us
  local copies, waits for them, and re-layouts: 34 us -> 2.53 us
  other arithmetic: 29 us -> 0 us
  starting transfers between devices: 15.6 us -> 0 us
    pallas_call x0 -> x1, Pallas kernels: none -> 50.7 us  [local(): pl.pallas_call(functools.partial(kernel, size, structs), out_shape=(jax.S...]
    psum x2 -> x0, blocking collectives: 41.2 us -> none  [the longest x1 31.6 us: local(): virial, counts = lax.psum((virial, counts), 'atom')]
    dot_general x5 -> x0, matrix products: 33.5 us -> none  [the longest x1 9.7 us: radial_terms(): dradial = jnp.dot(radial_out, dhidden, preferred_element_type=jnp.float32)]
    gather x3 -> x0, local copies, waits for them, and re-layouts: 28.7 us -> none  [the longest x1 17.3 us: local(): far_feat = whole_feat[:, flat_index]]
    all_gather x3 -> x0, blocking collectives: 24.7 us -> none  [the longest x1 9.87 us: local(): lax.all_gather(mixing, 'chan', axis=1, tiled=True)]
    scatter-add x2 -> x0, other arithmetic: 23.2 us -> none  [the longest x1 22.5 us: local(): jnp.zeros((3, atom_count + 2 * RIM), jnp.float32).at[:, flat_index]]
    ppermute x6 -> x0, starting transfers between devices: 15.6 us -> none  [the longest x2 8.75 us: with_halo(): before = lax.ppermute(last, axis, up)]
  transfers between devices with their start and end apart: 6 -> 0, of which waited for: 0 -> 0; matrix products, arithmetic and copies ran while one was open for 13% -> 0% of each run, Pallas kernels for 0% -> 0%
where the time goes in v1:
time: 54.1 us; the launch traced here: 53.9 us
  Pallas kernels  50.7 us (94%)
  local copies, waits for them, and re-layouts  2.53 us (5%)
  between operations  0.65 us (1%)
    pallas_call x1, Pallas kernels, local(): pl.pallas_call(functools.partial(kernel, size, structs), out_shape=(jax.S...  50.7 us
    unnamed x4, local copies, waits for them, and re-layouts  2.53 us

profile of v1, /device:TPU:0, one launch (start us, length us, event | category | flops | bytes accessed | tf_op | source)
XLA Modules:
  0.0 53.9 jit_solution(1428965872023621314)
XLA Ops:
  0.6 50.7 %shard_map.104 = (f32[3,128]{1,0:T(4,128)}, f32[9,16]{1,0:T(8,128)}) custom-call(f32[3,128]{1,0:T(4,128)} %pos.1, bf16[256,128]{1,0:T(8,128)(2,1)} %feat.1, s32[1,128]{1,0:T(1,128)} %bitcast.3, s32[64,128]{1,0:T(8,128)} %slots.1, s32[64,128]{1,0:T(8,128)} %valid.1, bf16[512,128]{1,0:T(8,128)(2,1)} %r_in.1, bf16[256,512]{1,0:T(8,128)(2,1)} %r_out.1, ...), custom_call_target="tpu_custom_call" | custom-call | tf_op jit(solution)/shard_map/pallas_call | solution.py:335
  51.3 0.0 copy-start
  51.3 0.7 %copy-done = f32[3,128]{1,0:T(4,128)S(1)} copy-done((f32[3,128]{1,0:T(4,128)S(1)}, f32[3,128]{1,0:T(4,128)}, u32[]{:S(2)}) %copy-start) | copy-done | bytes 1560
  52.0 0.6 %copy.13 = f32[3,128]{1,0:T(4,128)} copy(f32[3,128]{1,0:T(4,128)S(1)} %copy-done) | data formatting | bytes 3072
  52.6 1.3 %copy.14 = f32[9,16]{1,0:T(8,128)} copy(f32[9,16]{1,0:T(8,128)} %get-tuple-element.5) | data formatting | bytes 1152
Async XLA Ops:
  51.3 0.7 %copy-start = (f32[3,128]{1,0:T(4,128)S(1)}, f32[3,128]{1,0:T(4,128)}, u32[]{:S(2)}) copy-start(f32[3,128]{1,0:T(4,128)} %get-tuple-element.4) | copy-start | bytes 4612

commit v2 on v1

--- a/solution.py
+++ b/solution.py
@@ -12,7 +12,7 @@
 reach = 10.0
 F32 = jnp.float32
 BF16 = jnp.bfloat16
-TILE = 256
+TILE = 512
 MESH = pl.DeviceIdType.MESH
 
 

time: 54.1 us -> 45 us (0.83)
  Pallas kernels: 50.7 us -> 41.6 us
    pallas_call x1, Pallas kernels: 50.7 us -> 41.6 us  [local(): pl.pallas_call(functools.partial(kernel, size, structs), out_shape=(jax.S...]
where the time goes in v2:
time: 45 us; the launch traced here: 44.8 us
  Pallas kernels  41.6 us (92%)
  local copies, waits for them, and re-layouts  2.53 us (6%)
  between operations  0.65 us (1%)
    pallas_call x1, Pallas kernels, local(): pl.pallas_call(functools.partial(kernel, size, structs), out_shape=(jax.S...  41.6 us
    unnamed x4, local copies, waits for them, and re-layouts  2.53 us

profile of v2, /device:TPU:0, one launch (start us, length us, event | category | flops | bytes accessed | tf_op | source)
XLA Modules:
  0.0 44.8 jit_solution(3713381453891437135)
XLA Ops:
  0.6 41.6 %shard_map.104 = (f32[3,128]{1,0:T(4,128)}, f32[9,16]{1,0:T(8,128)}) custom-call(f32[3,128]{1,0:T(4,128)} %pos.1, bf16[256,128]{1,0:T(8,128)(2,1)} %feat.1, s32[1,128]{1,0:T(1,128)} %bitcast.3, s32[64,128]{1,0:T(8,128)} %slots.1, s32[64,128]{1,0:T(8,128)} %valid.1, bf16[512,128]{1,0:T(8,128)(2,1)} %r_in.1, bf16[256,512]{1,0:T(8,128)(2,1)} %r_out.1, ...), custom_call_target="tpu_custom_call" | custom-call | tf_op jit(solution)/shard_map/pallas_call | solution.py:335
  42.3 0.0 copy-start
  42.3 0.7 %copy-done = f32[3,128]{1,0:T(4,128)S(1)} copy-done((f32[3,128]{1,0:T(4,128)S(1)}, f32[3,128]{1,0:T(4,128)}, u32[]{:S(2)}) %copy-start) | copy-done | bytes 1560
  42.9 0.6 %copy.13 = f32[3,128]{1,0:T(4,128)} copy(f32[3,128]{1,0:T(4,128)S(1)} %copy-done) | data formatting | bytes 3072
  43.5 1.3 %copy.14 = f32[9,16]{1,0:T(8,128)} copy(f32[9,16]{1,0:T(8,128)} %get-tuple-element.5) | data formatting | bytes 1152
Async XLA Ops:
  42.3 0.7 %copy-start = (f32[3,128]{1,0:T(4,128)S(1)}, f32[3,128]{1,0:T(4,128)}, u32[]{:S(2)}) copy-start(f32[3,128]{1,0:T(4,128)} %get-tuple-element.4) | copy-start | bytes 4612

commit v3 on v2

--- a/solution.py
+++ b/solution.py
@@ -27,6 +27,17 @@
 def kernel(
     size,
     structs,
+    pos_h,
+    feat_h,
+    sid_h,
+    slots_h,
+    valid_h,
+    r_in_h,
+    r_out_h,
+    mix_h,
+    readout_h,
+    forces,
+    stress,
     pos,
     feat,
     sid,
@@ -36,8 +47,6 @@
     r_out,
     mix,
     readout,
-    forces,
-    stress,
     fwin,
     pnbr,
     ro_r,
@@ -71,6 +80,7 @@
     mix_sems,
     psems,
     tsems,
+    load_sems,
 ):
     a, c = lax.axis_index("atom"), lax.axis_index("chan")
     channels, atoms = feat.shape
@@ -97,6 +107,13 @@
     barrier = pltpu.get_barrier_semaphore()
     for atom, chan in plane + line + ends:
         pl.semaphore_signal(barrier, inc=1, device_id=at(atom, chan), device_id_type=MESH)
+    given = (pos_h, feat_h, slots_h, valid_h, mix_h, r_in_h, r_out_h, readout_h, sid_h)
+    held = (pos, feat, slots, valid, mix, r_in, r_out, readout, sid)
+    loads = [
+        pltpu.make_async_copy(src, dst, load_sems.at[k]) for k, (src, dst) in enumerate(zip(given, held))
+    ]
+    for load in loads:
+        load.start()
     pl.semaphore_wait(barrier, len(plane) + len(line) + len(ends))
 
     def send(src, dst, sem, sem_recv, atom, chan):
@@ -114,21 +131,24 @@
     nbr = pl.ds(atoms, atoms)
     own = pl.ds(0, atoms)
     started = [
-        send(pos, pnbr, pos_sems.at[0], pos_sems.at[1], jnp.where(early, after, before), c)
+        send(pos_h, pnbr, pos_sems.at[0], pos_sems.at[1], jnp.where(early, after, before), c)
     ]
-    for chan in range(n):
-        rel = lax.rem(c - chan + n, n)
-        side = after if chan < n // 2 else before
+    for k in range(n):
+        chan = lax.rem(c + k, n)
+        rel = (n - k) % n
+        side = jnp.where(chan < n // 2, after, before)
         started.append(
-            send(feat, fwin.at[rel, :, nbr], nbr_sems.at[0, chan], nbr_sems.at[1, rel], side, chan)
+            send(feat_h, fwin.at[rel, :, nbr], nbr_sems.at[0, k], nbr_sems.at[1, rel], side, chan)
         )
     for k, chan in others:
         started.append(
-            send(feat, fwin.at[n - k, :, own], own_sems.at[0, k], own_sems.at[1, n - k], a, chan)
+            send(feat_h, fwin.at[n - k, :, own], own_sems.at[0, k], own_sems.at[1, n - k], a, chan)
         )
     for k, chan in others:
-        started.append(send(r_out, ro_r.at[n - k - 1], ro_sems.at[0, k], ro_sems.at[1, n - k], a, chan))
-        started.append(send(mix, mix_r.at[n - k - 1], mix_sems.at[0, k], mix_sems.at[1, n - k], a, chan))
+        started.append(send(r_out_h, ro_r.at[n - k - 1], ro_sems.at[0, k], ro_sems.at[1, n - k], a, chan))
+        started.append(send(mix_h, mix_r.at[n - k - 1], mix_sems.at[0, k], mix_sems.at[1, n - k], a, chan))
+    for load in loads:
+        load.wait()
 
     fwin[0, :, 0:atoms] = feat[...]
     lane = lax.broadcasted_iota(jnp.int32, (rows, atoms), 1)
@@ -338,9 +358,18 @@
             jax.ShapeDtypeStruct((3, atoms), F32),
             jax.ShapeDtypeStruct((9, structs), F32),
         ),
-        in_specs=[pl.BlockSpec(memory_space=vmem)] * 9,
+        in_specs=[pl.BlockSpec(memory_space=pl.ANY)] * 9,
         out_specs=(pl.BlockSpec(memory_space=vmem),) * 2,
         scratch_shapes=[
+            vmem((3, atoms), F32),
+            vmem((channels, atoms), BF16),
+            vmem((1, atoms), jnp.int32),
+            vmem((slot_count, atoms), jnp.int32),
+            vmem((slot_count, atoms), jnp.int32),
+            vmem(radial_in.shape, BF16),
+            vmem(radial_out.shape, BF16),
+            vmem(mixing.shape, BF16),
+            vmem((1, n * channels), F32),
             vmem((n, channels, 2 * atoms), BF16),
             vmem((3, atoms), F32),
             vmem((n - 1, channels, hidden), BF16),
@@ -374,6 +403,7 @@
             dma((2, n)),
             dma((4, max(plane, deep))),
             dma((4, n)),
+            dma((9,)),
         ],
         compiler_params=pltpu.CompilerParams(
             collective_id=0, has_side_effects=True, vmem_limit_bytes=60 * 1024 * 1024

time: 45 us -> 44.1 us (0.980)
  Pallas kernels: 41.6 us -> 40.7 us
    pallas_call x1, Pallas kernels: 41.6 us -> 40.7 us  [local(): pl.pallas_call(functools.partial(kernel, size, structs), out_shape=(jax.S...]
where the time goes in v3:
time: 44.1 us; the launch traced here: 43.9 us
  Pallas kernels  40.7 us (92%)
  local copies, waits for them, and re-layouts  2.53 us (6%)
  between operations  0.65 us (1%)
    pallas_call x1, Pallas kernels, local(): pl.pallas_call(functools.partial(kernel, size, structs), out_shape=(jax.S...  40.7 us
    unnamed x4, local copies, waits for them, and re-layouts  2.53 us

profile of v3, /device:TPU:0, one launch (start us, length us, event | category | flops | bytes accessed | tf_op | source)
XLA Modules:
  0.0 43.9 jit_solution(2985664253663971500)
XLA Ops:
  0.6 40.7 %shard_map.104 = (f32[3,128]{1,0:T(4,128)}, f32[9,16]{1,0:T(8,128)}) custom-call(f32[3,128]{1,0:T(4,128)} %pos_h.1, bf16[256,128]{1,0:T(8,128)(2,1)} %feat_h.1, s32[1,128]{1,0:T(1,128)} %bitcast.3, s32[64,128]{1,0:T(8,128)} %slots_h.1, s32[64,128]{1,0:T(8,128)} %valid_h.1, bf16[512,128]{1,0:T(8,128)(2,1)} %r_in_h.1, bf16[256,512]{1,0:T(8,128)(2,1)} %r_out_h.1, ...), custom_call_target="tpu_custom_call" | custom-call | tf_op jit(solution)/shard_map/pallas_call | solution.py:355
  41.3 0.0 copy-start
  41.3 0.7 %copy-done = f32[3,128]{1,0:T(4,128)S(1)} copy-done((f32[3,128]{1,0:T(4,128)S(1)}, f32[3,128]{1,0:T(4,128)}, u32[]{:S(2)}) %copy-start) | copy-done | bytes 1560
  42.0 0.6 %copy.13 = f32[3,128]{1,0:T(4,128)} copy(f32[3,128]{1,0:T(4,128)S(1)} %copy-done) | data formatting | bytes 3072
  42.6 1.3 %copy.14 = f32[9,16]{1,0:T(8,128)} copy(f32[9,16]{1,0:T(8,128)} %get-tuple-element.5) | data formatting | bytes 1152
Async XLA Ops:
  41.3 0.7 %copy-start = (f32[3,128]{1,0:T(4,128)S(1)}, f32[3,128]{1,0:T(4,128)}, u32[]{:S(2)}) copy-start(f32[3,128]{1,0:T(4,128)} %get-tuple-element.4) | copy-start | bytes 4612

commit v4 on v3

--- a/solution.py
+++ b/solution.py
@@ -26,7 +26,6 @@
 
 def kernel(
     size,
-    structs,
     pos_h,
     feat_h,
     sid_h,
@@ -36,8 +35,7 @@
     r_out_h,
     mix_h,
     readout_h,
-    forces,
-    stress,
+    result,
     pos,
     feat,
     sid,
@@ -326,7 +324,7 @@
     force = tabs[0]
     for k in range(1, 2 * n):
         force = force + tabs[k]
-    forces[...] = force[0:3, :]
+    result[0:8, :] = force
 
     for k in range(1, deep):
         spot = lax.rem(z + k, deep)
@@ -334,10 +332,14 @@
     summed = totals[0]
     for k in range(1, deep):
         summed = summed + totals[k]
-    out = -summed[0:9, :] / summed[9:10, :]
-    stress[...] = out[:, 0:structs]
+    result[8:24, :] = -summed / summed[9:10, :]
     for copy in (*started, *sends):
         copy.wait_send()
+
+
+def unpack(result, forces, stress):
+    forces[...] = result[0 : forces.shape[0], :]
+    stress[...] = result[8 : 8 + stress.shape[0], 0 : stress.shape[1]]
 
 
 def local(positions, features, struct_ids, slots, validity, radial_in, radial_out, mixing, readout):
@@ -352,14 +354,11 @@
     plane = n * group
     vmem = pltpu.VMEM
     dma = pltpu.SemaphoreType.DMA
-    return pl.pallas_call(
-        functools.partial(kernel, size, structs),
-        out_shape=(
-            jax.ShapeDtypeStruct((3, atoms), F32),
-            jax.ShapeDtypeStruct((9, structs), F32),
-        ),
+    result = pl.pallas_call(
+        functools.partial(kernel, size),
+        out_shape=jax.ShapeDtypeStruct((24, atoms), F32),
         in_specs=[pl.BlockSpec(memory_space=pl.ANY)] * 9,
-        out_specs=(pl.BlockSpec(memory_space=vmem),) * 2,
+        out_specs=pl.BlockSpec(memory_space=vmem),
         scratch_shapes=[
             vmem((3, atoms), F32),
             vmem((channels, atoms), BF16),
@@ -419,6 +418,15 @@
         mixing,
         readout.reshape(1, n * channels),
     )
+    return pl.pallas_call(
+        unpack,
+        out_shape=(
+            jax.ShapeDtypeStruct((3, atoms), F32),
+            jax.ShapeDtypeStruct((9, structs), F32),
+        ),
+        in_specs=[pl.BlockSpec(memory_space=vmem)],
+        out_specs=(pl.BlockSpec(memory_space=vmem),) * 2,
+    )(result)
 
 
 def solution(mesh):

time: 44.1 us -> 42.8 us (0.971)
  local copies, waits for them, and re-layouts: 2.53 us -> 0 us
  Pallas kernels: 40.7 us -> 42 us
    unnamed x4 -> x0, local copies, waits for them, and re-layouts: 2.53 us -> none
    pallas_call x1 -> x2, Pallas kernels: 40.7 us -> 42 us  [the longest x1 40.7 us: local(): pl.pallas_call(functools.partial(kernel, size), out_shape=jax.ShapeDtypeS...]
where the time goes in v4:
time: 42.8 us; the launch traced here: 42.6 us
  Pallas kernels  42 us (98%)
  between operations  0.64 us (1%)
    pallas_call x1, Pallas kernels, local(): pl.pallas_call(functools.partial(kernel, size), out_shape=jax.ShapeDtypeS...  40.7 us
    pallas_call x1, Pallas kernels, local(): pl.pallas_call(unpack, out_shape=(jax.ShapeDtypeStruct((3, atoms), F32),...  1.31 us

profile of v4, /device:TPU:0, one launch (start us, length us, event | category | flops | bytes accessed | tf_op | source)
XLA Modules:
  0.0 42.6 jit_solution(8213513926029143878)
XLA Ops:
  0.6 40.7 %shard_map.104.result = f32[24,128]{1,0:T(8,128)} custom-call(f32[3,128]{1,0:T(4,128)} %pos_h.1, bf16[256,128]{1,0:T(8,128)(2,1)} %feat_h.1, s32[1,128]{1,0:T(1,128)} %bitcast.3, s32[64,128]{1,0:T(8,128)} %slots_h.1, s32[64,128]{1,0:T(8,128)} %valid_h.1, bf16[512,128]{1,0:T(8,128)(2,1)} %r_in_h.1, bf16[256,512]{1,0:T(8,128)(2,1)} %r_out_h.1, ...), custom_call_target="tpu_custom_call" | custom-call | tf_op jit(solution)/shard_map/pallas_call | solution.py:357
  41.3 1.3 %shard_map.105 = (f32[3,128]{1,0:T(4,128)}, f32[9,16]{1,0:T(8,128)}) custom-call(f32[24,128]{1,0:T(8,128)} %shard_map.104.result), custom_call_target="tpu_custom_call" | custom-call | tf_op jit(solution)/shard_map/pallas_call | solution.py:421
